TPU v7x, 128 devices: a whole 4x4x4 slice. The times are simulated.
128 devices in a mesh: group: 4 (over x), bulk: 32 (over z, y, core).
Axes of the slice: x: 4, y: 4, z: 4, core: 2. Of those that a mesh axis runs over, the one named last changes fastest.
Arguments:
- rhs: float32 [512, 64, 128], P(('group', 'bulk')), may hold values from -90 to 90, as said below
- diag_tiles: float32 [512, 128, 128], P(('group', 'bulk')), may hold values from -0.06 to 0.06
- offdiag_blocks: float32 [512, 11, 128, 128], P(('group', 'bulk')), may hold values from -0.026 to 0.026
- coupling: float32 [256, 4, 128, 128], P(('group', 'bulk')), may hold values from -0.05 to 0.05, as said below
- col_index: int32 [512, 11], replicated, may hold values from 0 to 511, as said below
- load: int32 [512], replicated, may hold values from 3 to 11
- new_slot: int32 [512], replicated, may hold values from 0 to 511, as said below
Outputs:
- solution_out: float32 [512, 64, 128], P(('group', 'bulk'))
- residual_out: float32 [512, 64, 128], P(('group', 'bulk'))
Inputs may be any that keep to these rules, and one draw needn't show every extreme that they name: `rhs`: made of random entries times scales of the rows and of the columns. `coupling`: entry [d * 2 + k, h] is the transpose of entry [(h * 32 + d % 32) * 2 + k, d // 32]. `col_index`: for each part g and each tile position t, the column t of the 128 block rows of part g is a permutation of that part's slots g * 128 to (g + 1) * 128 - 1. Of the 44 entries of the 4 block rows of one device (slots d * 4 to (d + 1) * 4 - 1), at most 2 name slots of any one device, and exactly 2 name slots of some device. `new_slot`: A permutation. On every device exactly one block row moves, from a slot k with 2 <= k % 4; it stays in its part, goes from owner b to owner b XOR m, where m (1 to 31) is one number for the whole part, and takes the slot that the moving row of that device leaves.
All inputs are finite; a program needn't handle non-finite values.
Results may differ from a plain program's by a relative error of at most 0.0003.
Values sent between devices are 32-bit elements; how exact they have to be, the bound alone decides.
A program may use at most 64 MiB of HBM per device.

v0:
```python
import jax
import jax.numpy as jnp
from jax import lax
from jax.sharding import PartitionSpec as P

highest = lax.Precision.HIGHEST
diagonal_shift = 4.0


def from_partner(value, axis, bit):
    mask = 2**bit
    pairs = [(source, source ^ mask) for source in range(lax.axis_size(axis))]
    return lax.ppermute(value, axis, pairs)


def chol_apply(matrix, right):
    factor = jnp.linalg.cholesky(matrix)
    middle = lax.linalg.triangular_solve(factor, right, left_side=True, lower=True)
    return lax.linalg.triangular_solve(factor, middle, left_side=True, lower=True, transpose_a=True)


def global_gram(left, right):
    partial_gram = jnp.einsum("snt,smt->nm", left, right, precision=highest)
    total = lax.psum(partial_gram, ("group", "bulk"))
    return 0.5 * (total + total.T)


def operate(vectors, diag, masked, column_ids, coupling):
    row_count = vectors.shape[0]
    boundary_rows = coupling.shape[0]
    part_count = coupling.shape[1]
    group_rows = row_count * lax.axis_size("bulk")
    border = lax.all_gather(vectors[:boundary_rows], "group", axis=0, tiled=True)
    final_output = diagonal_shift * vectors + jnp.einsum(
        "rnj,rij->rni", vectors, diag, precision=highest
    )
    returned = jnp.einsum("rni,rkij->rknj", vectors, masked, precision=highest)
    flat_terms = returned.reshape((-1,) + vectors.shape[1:])
    panel = lax.all_gather(vectors, "bulk", axis=0, tiled=True)
    buffer = jax.ops.segment_sum(flat_terms, column_ids.reshape(-1), num_segments=group_rows)
    owed = lax.psum_scatter(buffer, "bulk", scatter_dimension=0, tiled=True)
    picked = panel[column_ids]
    final_output = (
        final_output + jnp.einsum("rknj,rkij->rni", picked, masked, precision=highest) + owed
    )
    border = border.reshape((part_count, boundary_rows) + vectors.shape[1:])
    crossed = jnp.einsum("khij,hknj->kni", coupling, border, precision=highest)
    return final_output.at[:boundary_rows].add(crossed)


def advance(state, diag, masked, column_ids, coupling, last_step):
    solution, resid, direction, gram_rr = state
    image = operate(direction, diag, masked, column_ids, coupling)
    gram_pq = global_gram(direction, image)
    alpha = chol_apply(gram_pq, gram_rr)
    solution = solution + jnp.einsum("mn,smt->snt", alpha, direction, precision=highest)
    resid = resid - jnp.einsum("mn,smt->snt", alpha, image, precision=highest)
    if not last_step:
        gram_new = global_gram(resid, resid)
        beta = chol_apply(gram_rr, gram_new)
        direction = resid + jnp.einsum("mn,smt->snt", beta, direction, precision=highest)
        gram_rr = gram_new
    return (solution, resid, direction, gram_rr)


def local(rhs, diag_tiles, offdiag_blocks, coupling, col_index, load, new_slot):
    row_count = rhs.shape[0]
    off_count = offdiag_blocks.shape[1]
    bulk_count = lax.axis_size("bulk")
    group_rows = row_count * bulk_count
    my_group = lax.axis_index("group")
    my_bulk = lax.axis_index("bulk")
    first_slot = (my_group * bulk_count + my_bulk) * row_count
    group_base = my_group * group_rows
    own_slots = first_slot + jnp.arange(row_count, dtype=jnp.int32)
    tile_ids = jnp.arange(off_count, dtype=jnp.int32)
    old_columns = col_index[own_slots] - group_base
    old_mask = (tile_ids[None, :] < load[own_slots][:, None]).astype(jnp.float32)
    old_masked = offdiag_blocks * old_mask[:, :, None, None]
    own_new = new_slot[own_slots]
    leaving = jnp.argmax((own_new != own_slots).astype(jnp.int32))
    target = own_new[leaving]
    target_bulk = target // row_count % bulk_count
    xor_mask = jnp.bitwise_xor(target_bulk, my_bulk)
    start_state = (jnp.zeros_like(rhs), rhs, rhs, global_gram(rhs, rhs))
    state = advance(start_state, diag_tiles, old_masked, old_columns, coupling, False)
    solution, resid, direction, gram_rr = state
    pieces = [
        offdiag_blocks[leaving],
        diag_tiles[leaving],
        solution[leaving],
        resid[leaving],
        direction[leaving],
    ]
    flat = jnp.concatenate([piece.reshape(-1) for piece in pieces])
    for bit_pos in range(bulk_count.bit_length() - 1):
        partner = from_partner(flat, "bulk", bit_pos)
        chosen = jnp.bitwise_and(jnp.right_shift(xor_mask, bit_pos), 1) == 1
        flat = jnp.where(chosen, partner, flat)
    outputs = []
    offset = 0
    for piece in pieces:
        outputs.append(flat[offset : offset + piece.size].reshape(piece.shape))
        offset = offset + piece.size
    moved_off = offdiag_blocks.at[leaving].set(outputs[0])
    moved_diag = diag_tiles.at[leaving].set(outputs[1])
    solution = solution.at[leaving].set(outputs[2])
    resid = resid.at[leaving].set(outputs[3])
    direction = direction.at[leaving].set(outputs[4])
    inverse = (
        jnp.zeros_like(new_slot).at[new_slot].set(jnp.arange(new_slot.shape[0], dtype=jnp.int32))
    )
    old_rows = inverse[own_slots]
    new_columns = new_slot[col_index[old_rows]] - group_base
    new_mask = (tile_ids[None, :] < load[old_rows][:, None]).astype(jnp.float32)
    new_masked = moved_off * new_mask[:, :, None, None]
    state = advance(
        (solution, resid, direction, gram_rr), moved_diag, new_masked, new_columns, coupling, True
    )
    return (state[0], state[1])


def solution(mesh):
    return jax.shard_map(
        local,
        mesh=mesh,
        in_specs=(
            P(("group", "bulk"), None, None),
            P(("group", "bulk"), None, None),
            P(("group", "bulk"), None, None, None),
            P(("group", "bulk"), None, None, None),
            P(),
            P(),
            P(),
        ),
        out_specs=(P(("group", "bulk"), None, None), P(("group", "bulk"), None, None)),
        check_vma=False,
    )
```

profile of v0, /device:TPU:1, one launch (start us, length us, event | category | flops | bytes accessed | tf_op | source)
XLA Modules:
  0.0 662.4 jit_solution(1041182074401895514)
XLA Ops:
  7.3 1.9 copy.86
  12.1 2.6 scatter_custom_fusion.1
  18.7 2.2 gather_fusion.5
  25.3 3.2 fusion.4
  28.5 2.5 broadcast.320.clone
  31.0 8.0 %scatter_fusion = f32[128,64,128]{2,1,0:T(8,128)} fusion(f32[128,64,128]{2,1,0:T(8,128)} %broadcast.320.clone, s32[44]{0:T(128)} %reshape.516, f32[44,64,128]{2,1,0:T(8,128)} %bitcast.222), kind=kCustom, calls=%fused_computation.9 | custom fusion | flops 360448 | bytes 4325552 | tf_op jit(solution)/shard_map/scatter-add | solution.py:40
  45.5 13.0 %all_gather.13 = f32[8,64,128]{2,1,0:T(8,128)} all-gather(f32[2,64,128]{2,1,0:T(8,128)} %slice.208), channel_id=1, replica_groups=mesh['group'=4,'bulk'=32] {'group'}, dimensions={0}, use_global_device_ids=true | all-gather | bytes 327680 | tf_op jit(solution)/shard_map/all_gather | solution.py:33
  62.4 4.0 gather_fusion.1
  66.4 5.4 fusion.12
  71.8 71.6 %reduce-scatter.3.cloned.1.call-done = f32[4,64,128]{2,1,0:T(8,128)} async-done(((f32[128,64,128]{2,1,0:T(8,128)}), f32[4,64,128]{2,1,0:T(8,128)}) %reduce-scatter.3.cloned.1.call-update) | async-done | bytes 131088 | tf_op jit(solution)/shard_map/reduce_scatter | solution.py:41
  143.4 1.7 fusion.21
  145.1 1.6 fusion.29
  148.2 66.3 %all-reduce = (f32[64,64]{1,0:T(8,128)}, f32[64,64]{1,0:T(8,128)}) all-reduce(f32[64,64]{1,0:T(8,128)} %convolution_bitcast_fusion.11, f32[64,64]{1,0:T(8,128)} %convolution_bitcast_fusion.12), channel_id=1, replica_groups=mesh['group'=4,'bulk'=32] {'group','bulk'}, use_global_device_ids=true, to_apply=%region_5.7 | all-reduce | flops 8192 | bytes 65536 | tf_op jit(solution)/shard_map/psum | solution.py:24
  224.5 7.2 %cholesky.59 = f32[64,64]{1,0:T(8,128)} custom-call(f32[64,64]{1,0:T(8,128)} %fusion.60), custom_call_target="Cholesky" | custom-call | tf_op jit(solution)/shard_map/jit(cholesky)/cholesky | solution.py:17
  233.2 2.1 fusion.36
  235.3 6.3 custom-call.13
  243.6 1.8 fusion.25
  247.7 7.2 %cholesky.70 = f32[64,64]{1,0:T(8,128)} custom-call(f32[64,64]{1,0:T(8,128)} %fusion.55), custom_call_target="Cholesky" | custom-call | tf_op jit(solution)/shard_map/jit(cholesky)/cholesky | solution.py:17
  256.4 2.1 fusion.37
  258.5 6.3 custom-call.15
  264.7 1.8 convolution_bitcast_fusion.9
  266.6 63.0 %psum.30 = f32[64,64]{1,0:T(8,128)} all-reduce(f32[64,64]{1,0:T(8,128)} %convolution_bitcast_fusion.9), channel_id=1, replica_groups=mesh['group'=4,'bulk'=32] {'group','bulk'}, use_global_device_ids=true, to_apply=%region_8.12 | all-reduce | flops 4096 | bytes 32768 | tf_op jit(solution)/shard_map/psum | solution.py:24
  341.3 2.2 broadcast_select_fusion
  344.7 20.3 %collective-permute-done.1 = f32[221184]{0:T(1024)} collective-permute-done((f32[221184]{0:T(1024)}, f32[221184]{0:T(1024)}, u32[]{:S(2)}, u32[]{:S(2)}) %collective-permute-start.1) | collective-permute-done | bytes 884768 | tf_op jit(solution)/shard_map/ppermute | solution.py:13
  365.0 2.2 broadcast_select_fusion.1
  367.2 2.9 collective-permute-start.2
  370.2 19.2 %collective-permute-done.2 = f32[221184]{0:T(1024)} collective-permute-done((f32[221184]{0:T(1024)}, f32[221184]{0:T(1024)}, u32[]{:S(2)}, u32[]{:S(2)}) %collective-permute-start.2) | collective-permute-done | bytes 884768 | tf_op jit(solution)/shard_map/ppermute | solution.py:13
  389.4 2.2 broadcast_select_fusion.2
  392.7 18.7 %collective-permute-done.3 = f32[221184]{0:T(1024)} collective-permute-done((f32[221184]{0:T(1024)}, f32[221184]{0:T(1024)}, u32[]{:S(2)}, u32[]{:S(2)}) %collective-permute-start.3) | collective-permute-done | bytes 884768 | tf_op jit(solution)/shard_map/ppermute | solution.py:13
  411.4 2.2 broadcast_select_fusion.3
  413.6 2.3 collective-permute-start.4
  416.7 17.4 %collective-permute-done.4 = f32[221184]{0:T(1024)} collective-permute-done((f32[221184]{0:T(1024)}, f32[221184]{0:T(1024)}, u32[]{:S(2)}, u32[]{:S(2)}) %collective-permute-start.4) | collective-permute-done | bytes 884768 | tf_op jit(solution)/shard_map/ppermute | solution.py:13
  436.2 2.0 fusion.40
  445.4 3.2 fusion
  448.6 2.5 broadcast.320
  451.1 7.8 %scatter_fusion.1 = f32[128,64,128]{2,1,0:T(8,128)} fusion(f32[128,64,128]{2,1,0:T(8,128)} %broadcast.320, s32[44]{0:T(128)S(1)} %broadcast_subtract_fusion.1, f32[44,64,128]{2,1,0:T(8,128)} %bitcast.223), kind=kCustom, calls=%fused_computation.11 | custom fusion | flops 360448 | bytes 4325552 | tf_op jit(solution)/shard_map/scatter-add | solution.py:40
  459.2 10.1 %all_gather.15 = f32[8,64,128]{2,1,0:T(8,128)} all-gather(f32[2,64,128]{2,1,0:T(8,128)S(1)} %slice.243), channel_id=1, replica_groups=mesh['group'=4,'bulk'=32] {'group'}, dimensions={0}, use_global_device_ids=true | all-gather | bytes 327680 | tf_op jit(solution)/shard_map/all_gather | solution.py:33
  469.3 2.1 fusion.35
  471.4 15.3 %all-gather.5.cloned.1.call-done = f32[128,64,128]{2,1,0:T(8,128)} async-done(((f32[4,64,128]{2,1,0:T(8,128)}), f32[128,64,128]{2,1,0:T(8,128)}) %all-gather.5.cloned.1.call-update) | async-done | bytes 4194320 | tf_op jit(solution)/shard_map/all_gather | solution.py:39
  486.7 4.0 gather_fusion.7
  490.7 5.4 fusion.15
  496.2 73.8 %reduce-scatter.5.cloned.1.call-done = f32[4,64,128]{2,1,0:T(8,128)} async-done(((f32[128,64,128]{2,1,0:T(8,128)}), f32[4,64,128]{2,1,0:T(8,128)}) %reduce-scatter.5.cloned.1.call-update) | async-done | bytes 131088 | tf_op jit(solution)/shard_map/reduce_scatter | solution.py:41
  570.0 1.7 fusion.19
  571.6 1.6 fusion.27
  573.5 66.0 %psum.31 = f32[64,64]{1,0:T(8,128)S(1)} all-reduce(f32[64,64]{1,0:T(8,128)S(1)} %convolution_bitcast_fusion.7), channel_id=1, replica_groups=mesh['group'=4,'bulk'=32] {'group','bulk'}, use_global_device_ids=true, to_apply=%region_13.17 | all-reduce | flops 4096 | bytes 32768 | tf_op jit(solution)/shard_map/psum | solution.py:24
  639.7 5.8 cholesky.81
  646.9 4.9 custom-call.17
  653.1 1.8 fusion.22
  (118 shorter events, 64.3 us)
Async XLA Ops:
  7.2 137.9 %copy-start = (f32[2,4,128,128]{3,2,1,0:T(8,128)S(1)}, f32[2,4,128,128]{3,2,1,0:T(8,128)}, u32[]{:S(2)}) copy-start(f32[2,4,128,128]{3,2,1,0:T(8,128)} %param.29) | copy-start | bytes 1572868
  7.2 18.1 %copy-start.3 = (f32[4,64,128]{2,1,0:T(8,128)S(1)}, f32[4,64,128]{2,1,0:T(8,128)}, u32[]{:S(2)}) copy-start(f32[4,64,128]{2,1,0:T(8,128)} %param.26) | copy-start | bytes 393220
  7.2 16.2 %copy-start.2 = (s32[512]{0:T(512)S(1)}, s32[512]{0:T(512)}, u32[]{:S(2)}) copy-start(s32[512]{0:T(512)} %param.31) | copy-start | bytes 6148
  7.2 4.3 copy-start.1
  7.2 55.2 %all-gather.3.cloned.1.call-start = ((), (), s32[]{:S(2)}) async-start(), calls=%async_computation.2 | async-start | bytes 4325376 | tf_op jit(solution)/shard_map/all_gather | solution.py:39
  7.3 1.9 copy-start.11
  9.9 133.5 %reduce-scatter.3.cloned.1.call-start = ((), (), s32[]{:S(2)}) async-start(), calls=%async_computation.3 | async-start | bytes 4325376 | tf_op jit(solution)/shard_map/reduce_scatter | solution.py:41
  39.0 447.7 %all-gather.5.cloned.1.call-start = ((), (), s32[]{:S(2)}) async-start(), calls=%async_computation.4 | async-start | bytes 4325376 | tf_op jit(solution)/shard_map/all_gather | solution.py:39
  71.8 266.4 %copy-start.13 = (s32[4]{0:T(128)S(1)}, s32[4]{0:T(128)}, u32[]{:S(2)}) copy-start(s32[4]{0:T(128)} %gather_fusion.3) | copy-start | bytes 52
  146.7 0.7 copy-start.7
  334.2 2.8 copy-start.4
  337.6 3.7 collective-permute-start
  343.5 21.5 %collective-permute-start.1 = (f32[221184]{0:T(1024)}, f32[221184]{0:T(1024)}, u32[]{:S(2)}, u32[]{:S(2)}) collective-permute-start(f32[221184]{0:T(1024)} %broadcast_select_fusion), channel_id=1, source_target_pairs={{0,2},{1,3},{2,0},{3,1},{4,6},{5,7},{6,4},{7,5},{8,10},{9,11},{10,... | collective-permute-start | bytes 2654216 | tf_op jit(solution)/shard_map/ppermute | solution.py:13
  367.2 48.7 %copy-start.14 = (s32[3]{0:T(128)S(1)}, s32[3]{0:T(128)}, u32[]{:S(2)}) copy-start(s32[3]{0:T(128)} %constant.237.clone.1) | copy-start | bytes 40
  367.2 49.5 %copy-start.8 = (f32[64,4,128]{2,0,1:T(8,128)S(1)}, f32[64,4,128]{2,0,1:T(8,128)}, u32[]{:S(2)}) copy-start(f32[64,4,128]{2,0,1:T(8,128)} %fusion.73) | copy-start | bytes 393220
  367.2 22.2 %collective-permute-start.2 = (f32[221184]{0:T(1024)}, f32[221184]{0:T(1024)}, u32[]{:S(2)}, u32[]{:S(2)}) collective-permute-start(f32[221184]{0:T(1024)} %broadcast_select_fusion.1), channel_id=1, source_target_pairs={{0,4},{1,5},{2,6},{3,7},{4,0},{5,1},{6,2},{7,3},{8,12},{9,13},{10,... | collective-permute-start | bytes 2654216 | tf_op jit(solution)/shard_map/ppermute | solution.py:13
  391.6 19.8 %collective-permute-start.3 = (f32[221184]{0:T(1024)}, f32[221184]{0:T(1024)}, u32[]{:S(2)}, u32[]{:S(2)}) collective-permute-start(f32[221184]{0:T(1024)} %broadcast_select_fusion.2), channel_id=1, source_target_pairs={{0,8},{1,9},{2,10},{3,11},{4,12},{5,13},{6,14},{7,15},{8,0},{9,1},... | collective-permute-start | bytes 2654216 | tf_op jit(solution)/shard_map/ppermute | solution.py:13
  392.7 47.8 %copy-start.12 = (s32[4,11,1]{1,0,2:T(4,128)S(1)}, s32[4,11,1]{1,0,2:T(4,128)}, u32[]{:S(2)}) copy-start(s32[4,11,1]{1,0,2:T(4,128)} %get-tuple-element.98) | copy-start | bytes 532
  413.6 20.5 %collective-permute-start.4 = (f32[221184]{0:T(1024)}, f32[221184]{0:T(1024)}, u32[]{:S(2)}, u32[]{:S(2)}) collective-permute-start(f32[221184]{0:T(1024)} %broadcast_select_fusion.3), channel_id=1, source_target_pairs={{0,16},{1,17},{2,18},{3,19},{4,20},{5,21},{6,22},{7,23},{8,24},{9,... | collective-permute-start | bytes 2654216 | tf_op jit(solution)/shard_map/ppermute | solution.py:13
  435.3 0.9 copy-start.6
  438.3 0.7 copy-start.9
  438.9 131.0 %reduce-scatter.5.cloned.1.call-start = ((), (), s32[]{:S(2)}) async-start(), calls=%async_computation.5 | async-start | bytes 4325376 | tf_op jit(solution)/shard_map/reduce_scatter | solution.py:41
  440.5 4.9 copy-start.5
  496.2 158.8 %copy-start.10 = (f32[4,64,128]{2,1,0:T(8,128)S(1)}, f32[4,64,128]{2,1,0:T(8,128)}, u32[]{:S(2)}) copy-start(f32[4,64,128]{2,1,0:T(8,128)} %copy-done.9) | copy-start | bytes 393220
Sparse Core Ops, SparseCore 0:
  10.3 49.7 all-gather.2
  63.7 79.6 reduce-scatter.2
  439.1 47.6 all-gather.4
  490.2 79.7 reduce-scatter.4
where the time goes:
time: 666 us; the launch traced here: 662 us
  waiting for transfers between devices  236 us (35%)
  blocking collectives  218 us (33%)
  other arithmetic  90.6 us (14%)
  local copies, waits for them, and re-layouts  50.3 us (8%)
  matrix products  39.5 us (6%)
  between operations  18.6 us (3%)
  starting transfers between devices  8.54 us (1%)
    psum x3, blocking collectives, global_gram(): total = lax.psum(partial_gram, ('group', 'bulk'))  195 us
    reduce_scatter x2, waiting for transfers between devices, operate(): owed = lax.psum_scatter(buffer, 'bulk', scatter_dimension=0, tiled=True)  145 us
    ppermute x5, waiting for transfers between devices, from_partner(): return lax.ppermute(value, axis, pairs)  75.6 us
    another operation x9, other arithmetic, chol_apply(): factor = jnp.linalg.cholesky(matrix)  23.9 us
    all_gather x2, blocking collectives, operate(): lax.all_gather(vectors[:boundary_rows], 'group', axis=0, tiled=True)  23.1 us
    another operation x6, other arithmetic, chol_apply(): lax.linalg.triangular_solve(factor, middle, left_side=True, lower=True, t...  22.2 us
    scatter-add x2, other arithmetic, operate(): jax.ops.segment_sum(flat_terms, column_ids.reshape(-1), num_segments=grou...  15.8 us
    all_gather x2, waiting for transfers between devices, operate(): panel = lax.all_gather(vectors, 'bulk', axis=0, tiled=True)  15.3 us
  transfers between devices with their start and end apart: 9, of which 7 were waited for; matrix products, arithmetic and copies ran while one was open for 12% of the time, Pallas kernels for 0%

commit v1 on v0

--- a/solution.py
+++ b/solution.py
@@ -21,7 +21,7 @@
 
 def global_gram(left, right):
     partial_gram = jnp.einsum("snt,smt->nm", left, right, precision=highest)
-    total = lax.psum(partial_gram, ("group", "bulk"))
+    total = lax.psum(lax.psum(partial_gram, "bulk"), "group")
     return 0.5 * (total + total.T)
 
 

time: 666 us -> 894 us (1.34)
  blocking collectives: 218 us -> 434 us
    psum x3 -> x6, blocking collectives: 195 us -> 410 us  [global_gram(): total = lax.psum(lax.psum(partial_gram, 'bulk'), 'group')]
  transfers between devices with their start and end apart: 9 -> 9, of which waited for: 7 -> 7; matrix products, arithmetic and copies ran while one was open for 12% -> 9% of each run, Pallas kernels for 0% -> 0%
where the time goes in v1:
time: 894 us; the launch traced here: 883 us
  blocking collectives  434 us (49%)
  waiting for transfers between devices  241 us (27%)
  other arithmetic  90.6 us (10%)
  local copies, waits for them, and re-layouts  50.3 us (6%)
  matrix products  38.6 us (4%)
  between operations  18.6 us (2%)
  starting transfers between devices  9.3 us (1%)
    psum x6, blocking collectives, global_gram(): total = lax.psum(lax.psum(partial_gram, 'bulk'), 'group')  410 us
    reduce_scatter x2, waiting for transfers between devices, operate(): owed = lax.psum_scatter(buffer, 'bulk', scatter_dimension=0, tiled=True)  145 us
    ppermute x5, waiting for transfers between devices, from_partner(): return lax.ppermute(value, axis, pairs)  83.1 us
    another operation x9, other arithmetic, chol_apply(): factor = jnp.linalg.cholesky(matrix)  23.9 us
    all_gather x2, blocking collectives, operate(): lax.all_gather(vectors[:boundary_rows], 'group', axis=0, tiled=True)  23.3 us
    another operation x6, other arithmetic, chol_apply(): lax.linalg.triangular_solve(factor, middle, left_side=True, lower=True, t...  22.2 us
  transfers between devices with their start and end apart: 9, of which 7 were waited for; matrix products, arithmetic and copies ran while one was open for 9% of the time, Pallas kernels for 0%

profile of v1, /device:TPU:1, one launch (start us, length us, event | category | flops | bytes accessed | tf_op | source)
XLA Modules:
  0.0 882.6 jit_solution(7572151993584937753)
XLA Ops:
  7.3 1.9 copy.86
  12.1 2.6 scatter_custom_fusion.1
  18.7 2.2 gather_fusion.5
  25.3 3.2 fusion.4
  28.5 2.5 broadcast.320.clone
  31.0 8.0 scatter_fusion
  45.5 13.0 %all_gather.13 = f32[8,64,128]{2,1,0:T(8,128)} all-gather(f32[2,64,128]{2,1,0:T(8,128)} %slice.208), channel_id=1, replica_groups=mesh['group'=4,'bulk'=32] {'group'}, dimensions={0}, use_global_device_ids=true | all-gather | bytes 327680 | tf_op jit(solution)/shard_map/all_gather | solution.py:33
  62.4 4.0 gather_fusion.1
  66.4 5.4 fusion.12
  71.8 71.6 %reduce-scatter.3.cloned.1.call-done = f32[4,64,128]{2,1,0:T(8,128)} async-done(((f32[128,64,128]{2,1,0:T(8,128)}), f32[4,64,128]{2,1,0:T(8,128)}) %reduce-scatter.3.cloned.1.call-update) | async-done | bytes 131088 | tf_op jit(solution)/shard_map/reduce_scatter | solution.py:41
  143.4 1.7 fusion.21
  148.2 121.1 %all-reduce = (f32[64,64]{1,0:T(8,128)}, f32[64,64]{1,0:T(8,128)}) all-reduce(f32[64,64]{1,0:T(8,128)} %convolution_bitcast_fusion.11, f32[64,64]{1,0:T(8,128)} %convolution_bitcast_fusion.12), channel_id=1, replica_groups=mesh['group'=4,'bulk'=32] {'bulk'}, use_global_device_ids=true, to_apply=%region_6.8 | all-reduce | flops 8192 | bytes 65536 | tf_op jit(solution)/shard_map/psum | solution.py:24
  269.3 14.8 %all-reduce.1 = (f32[64,64]{1,0:T(8,128)}, f32[64,64]{1,0:T(8,128)}) all-reduce(f32[64,64]{1,0:T(8,128)} %get-tuple-element.91, f32[64,64]{1,0:T(8,128)} %get-tuple-element.92), channel_id=1, replica_groups=mesh['group'=4,'bulk'=32] {'group'}, use_global_device_ids=true, to_apply=%region_7.9 | all-reduce | flops 8192 | bytes 65536 | tf_op jit(solution)/shard_map/psum | solution.py:24
  294.0 7.2 cholesky.59
  302.7 2.1 fusion.36
  304.8 6.3 custom-call.13
  313.1 1.8 fusion.25
  317.2 7.2 cholesky.70
  325.9 2.1 fusion.37
  328.0 6.3 custom-call.15
  334.3 1.8 convolution_bitcast_fusion.9
  336.1 128.1 %psum.60 = f32[64,64]{1,0:T(8,128)} all-reduce(f32[64,64]{1,0:T(8,128)} %convolution_bitcast_fusion.9), channel_id=1, replica_groups=mesh['group'=4,'bulk'=32] {'bulk'}, use_global_device_ids=true, to_apply=%region_10.14 | all-reduce | flops 4096 | bytes 32768 | tf_op jit(solution)/shard_map/psum | solution.py:24
  464.2 12.1 %psum.61 = f32[64,64]{1,0:T(8,128)} all-reduce(f32[64,64]{1,0:T(8,128)} %psum.60), channel_id=1, replica_groups=mesh['group'=4,'bulk'=32] {'group'}, use_global_device_ids=true, to_apply=%region_11.15 | all-reduce | flops 4096 | bytes 32768 | tf_op jit(solution)/shard_map/psum | solution.py:24
  484.3 9.1 %collective-permute-start = (f32[221184]{0:T(1024)}, f32[221184]{0:T(1024)}, u32[]{:S(2)}, u32[]{:S(2)}) collective-permute-start(f32[221184]{0:T(1024)} %bitcast_dynamic-update-slice_fusion.1), channel_id=1, source_target_pairs={{0,1},{1,0},{2,3},{3,2},{4,5},{5,4},{6,7},{7,6},{8,9},{9,8},{10,11... | collective-permute-start | bytes 2654216 | tf_op jit(solution)/shard_map/ppermute | solution.py:13
  496.5 2.2 broadcast_select_fusion
  498.7 21.5 %collective-permute-done.1 = f32[221184]{0:T(1024)} collective-permute-done((f32[221184]{0:T(1024)}, f32[221184]{0:T(1024)}, u32[]{:S(2)}, u32[]{:S(2)}) %collective-permute-start.1) | collective-permute-done | bytes 884768 | tf_op jit(solution)/shard_map/ppermute | solution.py:13
  520.3 2.2 broadcast_select_fusion.1
  522.5 22.2 %collective-permute-done.2 = f32[221184]{0:T(1024)} collective-permute-done((f32[221184]{0:T(1024)}, f32[221184]{0:T(1024)}, u32[]{:S(2)}, u32[]{:S(2)}) %collective-permute-start.2) | collective-permute-done | bytes 884768 | tf_op jit(solution)/shard_map/ppermute | solution.py:13
  544.6 2.2 broadcast_select_fusion.2
  546.9 19.8 %collective-permute-done.3 = f32[221184]{0:T(1024)} collective-permute-done((f32[221184]{0:T(1024)}, f32[221184]{0:T(1024)}, u32[]{:S(2)}, u32[]{:S(2)}) %collective-permute-start.3) | collective-permute-done | bytes 884768 | tf_op jit(solution)/shard_map/ppermute | solution.py:13
  566.7 2.2 broadcast_select_fusion.3
  569.6 19.7 %collective-permute-done.4 = f32[221184]{0:T(1024)} collective-permute-done((f32[221184]{0:T(1024)}, f32[221184]{0:T(1024)}, u32[]{:S(2)}, u32[]{:S(2)}) %collective-permute-start.4) | collective-permute-done | bytes 884768 | tf_op jit(solution)/shard_map/ppermute | solution.py:13
  591.5 2.0 fusion.40
  600.5 3.2 fusion
  603.6 2.5 broadcast.320
  606.1 7.8 scatter_fusion.1
  614.2 10.3 %all_gather.15 = f32[8,64,128]{2,1,0:T(8,128)} all-gather(f32[2,64,128]{2,1,0:T(8,128)S(1)} %slice.243), channel_id=1, replica_groups=mesh['group'=4,'bulk'=32] {'group'}, dimensions={0}, use_global_device_ids=true | all-gather | bytes 327680 | tf_op jit(solution)/shard_map/all_gather | solution.py:33
  624.5 2.1 fusion.35
  626.6 12.9 %all-gather.5.cloned.1.call-done = f32[128,64,128]{2,1,0:T(8,128)} async-done(((f32[4,64,128]{2,1,0:T(8,128)}), f32[128,64,128]{2,1,0:T(8,128)}) %all-gather.5.cloned.1.call-update) | async-done | bytes 4194320 | tf_op jit(solution)/shard_map/all_gather | solution.py:39
  639.5 4.0 gather_fusion.7
  643.5 5.4 fusion.15
  649.0 73.8 %reduce-scatter.5.cloned.1.call-done = f32[4,64,128]{2,1,0:T(8,128)} async-done(((f32[128,64,128]{2,1,0:T(8,128)}), f32[4,64,128]{2,1,0:T(8,128)}) %reduce-scatter.5.cloned.1.call-update) | async-done | bytes 131088 | tf_op jit(solution)/shard_map/reduce_scatter | solution.py:41
  722.8 1.7 fusion.19
  724.4 1.6 fusion.27
  726.3 120.9 %psum.62 = f32[64,64]{1,0:T(8,128)S(1)} all-reduce(f32[64,64]{1,0:T(8,128)S(1)} %convolution_bitcast_fusion.7), channel_id=1, replica_groups=mesh['group'=4,'bulk'=32] {'bulk'}, use_global_device_ids=true, to_apply=%region_16.20 | all-reduce | flops 4096 | bytes 32768 | tf_op jit(solution)/shard_map/psum | solution.py:24
  847.2 13.4 %psum.63 = f32[64,64]{1,0:T(8,128)S(1)} all-reduce(f32[64,64]{1,0:T(8,128)S(1)} %psum.62), channel_id=1, replica_groups=mesh['group'=4,'bulk'=32] {'group'}, use_global_device_ids=true, to_apply=%region_17.21 | all-reduce | flops 4096 | bytes 32768 | tf_op jit(solution)/shard_map/psum | solution.py:24
  860.8 5.8 cholesky.81
  868.0 4.9 custom-call.17
  (123 shorter events, 63.7 us)
Async XLA Ops:
  7.2 137.9 %copy-start = (f32[2,4,128,128]{3,2,1,0:T(8,128)S(1)}, f32[2,4,128,128]{3,2,1,0:T(8,128)}, u32[]{:S(2)}) copy-start(f32[2,4,128,128]{3,2,1,0:T(8,128)} %param.29) | copy-start | bytes 1572868
  7.2 18.1 %copy-start.3 = (f32[4,64,128]{2,1,0:T(8,128)S(1)}, f32[4,64,128]{2,1,0:T(8,128)}, u32[]{:S(2)}) copy-start(f32[4,64,128]{2,1,0:T(8,128)} %param.26) | copy-start | bytes 393220
  7.2 16.2 %copy-start.2 = (s32[512]{0:T(512)S(1)}, s32[512]{0:T(512)}, u32[]{:S(2)}) copy-start(s32[512]{0:T(512)} %param.31) | copy-start | bytes 6148
  7.2 4.3 copy-start.1
  7.2 55.2 %all-gather.3.cloned.1.call-start = ((), (), s32[]{:S(2)}) async-start(), calls=%async_computation.2 | async-start | bytes 4325376 | tf_op jit(solution)/shard_map/all_gather | solution.py:39
  7.3 1.9 copy-start.12
  9.9 133.5 %reduce-scatter.3.cloned.1.call-start = ((), (), s32[]{:S(2)}) async-start(), calls=%async_computation.3 | async-start | bytes 4325376 | tf_op jit(solution)/shard_map/reduce_scatter | solution.py:41
  39.0 600.5 %all-gather.5.cloned.1.call-start = ((), (), s32[]{:S(2)}) async-start(), calls=%async_computation.4 | async-start | bytes 4325376 | tf_op jit(solution)/shard_map/all_gather | solution.py:39
  71.8 421.6 %copy-start.14 = (s32[4]{0:T(128)S(1)}, s32[4]{0:T(128)}, u32[]{:S(2)}) copy-start(s32[4]{0:T(128)} %gather_fusion.3) | copy-start | bytes 52
  146.7 0.7 copy-start.8
  480.9 2.8 copy-start.4
  484.3 12.2 %collective-permute-start = (f32[221184]{0:T(1024)}, f32[221184]{0:T(1024)}, u32[]{:S(2)}, u32[]{:S(2)}) collective-permute-start(f32[221184]{0:T(1024)} %bitcast_dynamic-update-slice_fusion.1), channel_id=1, source_target_pairs={{0,1},{1,0},{2,3},{3,2},{4,5},{5,4},{6,7},{7,6},{8,9},{9,8},{10,11... | collective-permute-start | bytes 2654216 | tf_op jit(solution)/shard_map/ppermute | solution.py:13
  498.7 21.5 %collective-permute-start.1 = (f32[221184]{0:T(1024)}, f32[221184]{0:T(1024)}, u32[]{:S(2)}, u32[]{:S(2)}) collective-permute-start(f32[221184]{0:T(1024)} %broadcast_select_fusion), channel_id=1, source_target_pairs={{0,2},{1,3},{2,0},{3,1},{4,6},{5,7},{6,4},{7,5},{8,10},{9,11},{10,... | collective-permute-start | bytes 2654216 | tf_op jit(solution)/shard_map/ppermute | solution.py:13
  522.5 46.4 %copy-start.15 = (s32[3]{0:T(128)S(1)}, s32[3]{0:T(128)}, u32[]{:S(2)}) copy-start(s32[3]{0:T(128)} %constant.237.clone.1) | copy-start | bytes 40
  522.5 47.2 %copy-start.9 = (f32[64,4,128]{2,0,1:T(8,128)S(1)}, f32[64,4,128]{2,0,1:T(8,128)}, u32[]{:S(2)}) copy-start(f32[64,4,128]{2,0,1:T(8,128)} %fusion.73) | copy-start | bytes 393220
  522.5 22.2 %collective-permute-start.2 = (f32[221184]{0:T(1024)}, f32[221184]{0:T(1024)}, u32[]{:S(2)}, u32[]{:S(2)}) collective-permute-start(f32[221184]{0:T(1024)} %broadcast_select_fusion.1), channel_id=1, source_target_pairs={{0,4},{1,5},{2,6},{3,7},{4,0},{5,1},{6,2},{7,3},{8,12},{9,13},{10,... | collective-permute-start | bytes 2654216 | tf_op jit(solution)/shard_map/ppermute | solution.py:13
  546.8 19.8 %collective-permute-start.3 = (f32[221184]{0:T(1024)}, f32[221184]{0:T(1024)}, u32[]{:S(2)}, u32[]{:S(2)}) collective-permute-start(f32[221184]{0:T(1024)} %broadcast_select_fusion.2), channel_id=1, source_target_pairs={{0,8},{1,9},{2,10},{3,11},{4,12},{5,13},{6,14},{7,15},{8,0},{9,1},... | collective-permute-start | bytes 2654216 | tf_op jit(solution)/shard_map/ppermute | solution.py:13
  546.8 48.7 %copy-start.13 = (s32[4,11,1]{1,0,2:T(4,128)S(1)}, s32[4,11,1]{1,0,2:T(4,128)}, u32[]{:S(2)}) copy-start(s32[4,11,1]{1,0,2:T(4,128)} %get-tuple-element.100) | copy-start | bytes 532
  568.9 20.5 %collective-permute-start.4 = (f32[221184]{0:T(1024)}, f32[221184]{0:T(1024)}, u32[]{:S(2)}, u32[]{:S(2)}) collective-permute-start(f32[221184]{0:T(1024)} %broadcast_select_fusion.3), channel_id=1, source_target_pairs={{0,16},{1,17},{2,18},{3,19},{4,20},{5,21},{6,22},{7,23},{8,24},{9,... | collective-permute-start | bytes 2654216 | tf_op jit(solution)/shard_map/ppermute | solution.py:13
  590.6 0.9 copy-start.7
  593.5 0.7 copy-start.10
  594.2 128.6 %reduce-scatter.5.cloned.1.call-start = ((), (), s32[]{:S(2)}) async-start(), calls=%async_computation.5 | async-start | bytes 4325376 | tf_op jit(solution)/shard_map/reduce_scatter | solution.py:41
  595.5 4.9 copy-start.5
  649.0 225.2 %copy-start.6 = (f32[4,64,128]{2,1,0:T(8,128)S(1)}, f32[4,64,128]{2,1,0:T(8,128)}, u32[]{:S(2)}) copy-start(f32[4,64,128]{2,1,0:T(8,128)} %get-tuple-element.97) | copy-start | bytes 393220
  649.0 226.1 %copy-start.11 = (f32[4,64,128]{2,1,0:T(8,128)S(1)}, f32[4,64,128]{2,1,0:T(8,128)}, u32[]{:S(2)}) copy-start(f32[4,64,128]{2,1,0:T(8,128)} %copy-done.10) | copy-start | bytes 393220
Sparse Core Ops, SparseCore 0:
  10.3 49.7 all-gather.2
  63.7 79.6 reduce-scatter.2
  594.3 45.1 all-gather.4
  643.0 79.7 reduce-scatter.4
